TPU v7x, 512 devices: a whole 4x8x8 slice. The times are simulated.
512 devices in a mesh: lat: 32 (over x, z), lon: 16 (over y, core).
Axes of the slice: x: 4, y: 8, z: 8, core: 2. Of those that a mesh axis runs over, the one named last changes fastest.
Arguments:
- tangent: float32 [256, 3, 128, 2048], P(None, None, 'lat', 'lon'), may hold values from -40 to 40
- base_state: float32 [4, 128, 2048], P(None, 'lat', 'lon'), may hold values from -0.4 to 0.8
Outputs:
- fields: float32 [256, 3, 128, 2048], P(None, None, 'lat', 'lon')
- upper: float32 [256, 256], replicated
All inputs are finite; a program needn't handle non-finite values.
Results may differ from a plain program's by a relative error of at most 0.00012.
Values sent between devices are 32-bit elements; how exact they have to be, the bound alone decides.
No kernel may reach another device: no remote copies, remote signals or barrier semaphores. Data moves between devices by JAX's collectives and lax.ppermute only.
A program may use at most 64 MiB of HBM per device.

v0:
```python
import jax
import jax.numpy as jnp
from jax import lax
from jax.experimental import pallas as pl
from jax.experimental.pallas import tpu as pltpu
from jax.sharding import PartitionSpec as P


HI = lax.Precision.HIGHEST
F32 = jnp.float32


def iota(shape, dim):
    return lax.broadcasted_iota(jnp.int32, shape, dim)


def eight(i, base=0):
    at = base + 8 * i
    return pl.ds(at if isinstance(at, int) else pl.multiple_of(at, 8), 8)


def split_rows(x_hbm, base_hbm, low_ref, high_ref, pack_ref, x_ref, base_ref, sems):
    places = [pl.ds(768 * k, 768) for k in range(4)]
    copies = [pltpu.make_async_copy(x_hbm.at[p], x_ref.at[p], sems.at[k]) for k, p in enumerate(places)]
    base_copy = pltpu.make_async_copy(base_hbm, base_ref, sems.at[4])
    for copy in copies:
        copy.start()
    base_copy.start()
    lane = iota((8, 128), 1)
    slot = lane % 32
    field = lane // 32

    def packed(parts):
        acc = jnp.zeros((8, 128), F32)
        for f, r, part in parts:
            at = 32 * f + 8 * r
            moved = pltpu.roll(part, (at + 2) % 128, 1)
            acc = acc + jnp.where((field == f) & (slot >= 8 * r) & (slot < 8 * r + 4), moved, 0.0)
        return acc + pltpu.roll(acc, 4, 1)

    def chunk(i, carry):
        for half in range(2):
            parts = []
            for f in range(3):
                for r in range(4):
                    part = x_ref[pl.ds(192 * i + 96 * half + 4 * f + r, 8, stride=12), :]
                    ref = low_ref if r < 2 else high_ref
                    start = ((r % 2) * 3 + f) * 256
                    ref[pl.ds(pl.multiple_of(start + 16 * i + 8 * half, 8), 8), :] = part
                    parts.append((f, r, part))
            pack_ref[eight(2 * i + half), :] = packed(parts)
        return carry

    for k, copy in enumerate(copies):
        copy.wait()
        lax.fori_loop(4 * k, 4 * k + 4, chunk, 0, unroll=2)
    base_copy.wait()
    parts = []
    for r in range(4):
        rows = base_ref[pl.ds(r, 4, stride=4), :]
        both = jnp.concatenate([rows, rows], axis=0)
        parts.append((0, r, both))
        if r == 0:
            low_ref[1536:1544, :] = both
        if r == 3:
            high_ref[1536:1544, :] = both
    pack_ref[256:264, :] = packed(parts)


def corners_out(west_ref, east_ref, up_ref, down_ref):
    slot = iota((256, 128), 1) % 8
    joined = jnp.where(slot < 4, west_ref[0:256, :], east_ref[0:256, :])
    row = iota((8, 128), 0)
    lane = iota((8, 128), 1)
    for ref, r in ((up_ref, 3), (down_ref, 0)):
        at = 32 * (row // 2) + 8 * r + jnp.where(row % 2 == 0, 1, 6)
        pick = jnp.where((lane == at) & (row < 6), 1.0, 0.0)
        ref[...] = lax.dot_general(
            pick, joined, (((1,), (1,)), ((), ())), precision=HI, preferred_element_type=F32
        )


def spread_corners(corner, r):
    row = iota((8, 128), 0)
    lane = iota((8, 128), 1)
    at = 32 * (row // 2) + 8 * r
    west = (row % 2 == 0) & (lane == at + 1)
    east = (row % 2 == 1) & ((lane == at) | (lane == at + 6))
    place = jnp.where((west | east) & (row < 6), 1.0, 0.0)
    return lax.dot_general(
        corner, place, (((0,), (0,)), ((), ())), precision=HI, preferred_element_type=F32
    )


def set_coefs(coef_ref, at, lines):
    for plane, line in enumerate(lines):
        coef_ref[4 * at + plane] = jnp.broadcast_to((1.0 if plane == 3 else 0.5) * line, (8, 128))


def edge_lines(pack_ref, west_ref, east_ref):
    slot = iota((1, 128), 1) % 8
    for plane in range(4):
        row = slice(256 + plane, 257 + plane)
        yield jnp.where(slot < 2, west_ref[row, :], jnp.where(slot >= 6, east_ref[row, :], pack_ref[row, :]))


def advanced(coef_ref, at, q, dx, dy):
    a, b, c, d = (coef_ref[4 * at + k] for k in range(4))
    h = q[0] - a * dx[0] - b * dy[0] - c * (dx[1] + dy[2])
    u = q[1] - a * dx[1] - b * dy[1] + d * q[2] - 0.25 * dx[0]
    v = q[2] - a * dx[2] - b * dy[2] - d * q[1] - 0.25 * dy[0]
    return [h, u, v]


def from_north(coef_ref, at, q):
    b, c = (coef_ref[4 * at + k] for k in (1, 2))
    return [-(b * q[0]) - c * q[2], -(b * q[1]), -(b * q[2]) - 0.25 * q[0]]


def minus(q):
    return [-x for x in q]


def plus(p, q):
    return [x + y for x, y in zip(p, q)]


def across(lane, x, ends, r):
    ends = pltpu.roll(ends, (127 - 8 * r) % 128, 1)
    east = jnp.where(lane == 127, ends, pltpu.roll(x, 127, 1))
    west = jnp.where(lane == 0, ends, pltpu.roll(x, 1, 1))
    return east - west


def beside(lane, edge):
    return jnp.where(lane % 8 == 0, pltpu.roll(edge, 122, 1), edge)


def by_field(x):
    return [x, pltpu.roll(x, 96, 1), pltpu.roll(x, 64, 1)]


def read_row(ref, r, i):
    return [ref[eight(i, (3 * r + f) * 256), :] for f in range(3)]


def own_part(
    base_ref, low_ref, high_ref, pack_ref, west_ref, east_ref, s_low_ref, s_high_ref, coef_ref, one_ref, ends_ref
):
    lane = iota((8, 128), 1)
    slot = lane % 8
    for r in range(4):
        set_coefs(coef_ref, r, [base_ref[4 * k + r:4 * k + r + 1, :] for k in range(4)])
    set_coefs(coef_ref, 4, edge_lines(pack_ref, west_ref, east_ref))

    def step(q, ends):
        out = []
        for r in range(4):
            dx = [across(lane, q[r][f], ends[f], r) for f in range(3)]
            if r == 0:
                dy = q[1]
            elif r == 3:
                dy = minus(q[2])
            else:
                dy = plus(q[r + 1], minus(q[r - 1]))
            out.append(advanced(coef_ref, r, q[r], dx, dy))
        return out

    def first(i, carry):
        q = [read_row(low_ref if r < 2 else high_ref, r % 2, i) for r in range(4)]
        at = eight(i)
        joined = jnp.where(slot < 2, west_ref[at, :], jnp.where(slot >= 6, east_ref[at, :], pack_ref[at, :]))
        edge = by_field(joined)
        one = step(q, [beside(lane, e) for e in edge])
        for r in range(4):
            for f in range(3):
                one_ref[3 * r + f, at, :] = one[r][f]
        dx = [pltpu.roll(e, 127, 1) - pltpu.roll(e, 1, 1) for e in edge]
        dy = [
            jnp.where(lane < 24, pltpu.roll(e, 120, 1), 0.0) - jnp.where(lane >= 8, pltpu.roll(e, 8, 1), 0.0)
            for e in edge
        ]
        for f, e in enumerate(advanced(coef_ref, 4, edge, dx, dy)):
            ends_ref[f, at, :] = beside(lane, e)
        return carry

    def second(i, carry):
        at = eight(i)
        one = [[one_ref[3 * r + f, at, :] for f in range(3)] for r in range(4)]
        two = step(one, [ends_ref[f, at, :] for f in range(3)])
        for r in range(4):
            ref = s_low_ref if r < 2 else s_high_ref
            for f in range(3):
                ref[3 * (r % 2) + f, at, :] = two[r][f]
        return carry

    lax.fori_loop(0, 32, first, 0, unroll=2)
    lax.fori_loop(0, 32, second, 0, unroll=8)


def add_side(north, inside, base_ref, half_ref, halo_ref, packs, corner_ref, part_ref, s_ref, coef_ref, spread_ref):
    lane = iota((8, 128), 1)
    sign = (lambda q: q) if north else minus
    near, far = (3, 2) if north else (0, 1)
    spread_ref[...] = spread_corners(corner_ref[...], near)
    set_coefs(coef_ref, 0, [base_ref[4 * k + near:4 * k + near + 1, :] for k in range(4)])
    set_coefs(coef_ref, 1, [base_ref[4 * k + far:4 * k + far + 1, :] for k in range(4)])
    set_coefs(coef_ref, 2, [halo_ref[1536 + k:1537 + k, :] for k in range(4)])
    set_coefs(coef_ref, 3, edge_lines(*packs))

    def gained_row(i):
        halo = read_row(halo_ref, 0 if north else 1, i)
        return halo, sign(from_north(coef_ref, 0, halo))

    def add(r, i, extra):
        for f in range(3):
            s_ref[3 * r + f, eight(i), :] = part_ref[3 * r + f, eight(i), :] + extra[f]

    def far_row(i):
        add(far % 2, i, sign(from_north(coef_ref, 1, gained_row(i)[1])))

    def near_row(i):
        own = read_row(half_ref, near % 2, i)
        halo, gained = gained_row(i)
        outer = read_row(halo_ref, 1 if north else 0, i)
        corner = by_field(spread_ref[eight(i), :])
        dx = [across(lane, halo[f], corner[f], near) for f in range(3)]
        dy = sign(plus(outer, minus(own)))
        beyond = [x * inside for x in advanced(coef_ref, 2, halo, dx, dy)]
        ends = [beside(lane, e) for e in sign(from_north(coef_ref, 3, corner))]
        dx = [across(lane, gained[f], ends[f], near) for f in range(3)]
        add(near % 2, i, advanced(coef_ref, 0, gained, dx, sign(beyond)))

    def chunk(i, carry):
        far_row(i)
        near_row(i)
        return carry

    if not north:
        lax.fori_loop(0, 32, chunk, 0, unroll=4)
        return gram_of_row(s_ref, 0) + gram_of_row(s_ref, 1)
    for i in range(32):
        far_row(i)
    total = gram_of_row(s_ref, far % 2)
    for i in range(32):
        near_row(i)
    return total + gram_of_row(s_ref, near % 2)


def gram_of_row(s_ref, r):
    row = jnp.concatenate([s_ref[3 * r + f] for f in range(3)], axis=1)
    return lax.dot_general(row, row, (((1,), (1,)), ((), ())), precision=HI, preferred_element_type=F32)


def south_side(
    inside_ref, base_ref, half_ref, halo_ref, pack_ref, west_ref, east_ref, corner_ref, part_ref,
    s_ref, gram_ref, coef_ref, spread_ref,
):
    gram_ref[...] = add_side(False, inside_ref[0].astype(F32), base_ref, half_ref, halo_ref, (pack_ref, west_ref, east_ref),
             corner_ref, part_ref, s_ref, coef_ref, spread_ref)


def north_side(
    inside_ref, base_ref, half_ref, halo_ref, pack_ref, west_ref, east_ref, corner_ref, part_ref, partial_ref,
    s_ref, gram_ref, coef_ref, spread_ref,
):
    total = add_side(True, inside_ref[1].astype(F32), base_ref, half_ref, halo_ref, (pack_ref, west_ref, east_ref),
             corner_ref, part_ref, s_ref, coef_ref, spread_ref)
    total = total + partial_ref[...]
    row = iota((128, 128), 0)
    col = iota((128, 128), 1)
    corner = total[128:, 128:]
    gram_ref[0:128, :] = jnp.where(row >= col, total[:128, :128], corner)
    gram_ref[128:256, :] = total[128:, :128]
    diagonal = jnp.sum(jnp.where(row == col, corner, 0.0), axis=0, keepdims=True)
    gram_ref[256:272, :] = jnp.where(iota((16, 128), 0) == 0, diagonal, 0.0)


def sum_copies(in_ref, out_ref):
    total = in_ref[0]
    for k in range(1, in_ref.shape[0]):
        total = total + in_ref[k]
    for k in range(out_ref.shape[0]):
        out_ref[k] = total


def lanes_of(x, lane):
    return jnp.broadcast_to(x[:, lane:lane + 1], x.shape)


def row_of(x, row):
    return jnp.broadcast_to(x[row:row + 1, :], x.shape)


def eliminate(m_ref):
    sub = iota((8, 128), 0)
    for panel in range(4):
        j0 = 64 * panel
        td = j0 // 128
        tiles = (0, 1, 2) if td == 0 else (1, 2, 3)
        rows = [{t: m_ref[j0 + 8 * g:j0 + 8 * g + 8, 128 * t:128 * t + 128] for t in tiles} for g in range(8)]
        for b in range(8):
            lane = j0 % 128 + 8 * b
            cols = [[lanes_of(rows[b][td], lane + m) for m in range(8)]]
            work = [dict(rows[g]) for g in range(b, 8)]
            pivot = row_of(cols[0][0], 0)
            steps = []
            for k in range(8):
                r = lax.rsqrt(pivot)
                inv = r * r
                scale = r if k == 0 else jnp.where(sub == k, r, scale)
                line = {m: row_of(cols[0][m], k) for m in range(k + 1, 8)}
                if k < 7:
                    pivot = row_of(cols[0][k + 1], k + 1) - (line[k + 1] * line[k + 1]) * inv
                wide = {t: row_of(work[0][t], k) for t in tiles}
                f = jnp.where(sub > k, cols[0][k] * inv, 0.0)
                for m in range(k + 1, 8):
                    cols[0][m] = cols[0][m] - f * line[m]
                for t in tiles:
                    work[0][t] = work[0][t] - f * wide[t]
                steps.append((inv, line, wide))
            for g in range(1, 8 - b):
                left = [lanes_of(rows[b + g][td], lane + m) for m in range(8)]
                for k, (inv, line, wide) in enumerate(steps):
                    f = left[k] * inv
                    for m in range(k + 1, 8):
                        left[m] = left[m] - f * line[m]
                    for t in tiles:
                        work[g][t] = work[g][t] - f * wide[t]
            for g in range(b, 8):
                rows[g] = work[g - b]
            for t in tiles:
                rows[b][t] = rows[b][t] * scale
                m_ref[j0 + 8 * b:j0 + 8 * b + 8, 128 * t:128 * t + 128] = rows[b][t]
        if panel == 3:
            break
        first = j0 + 64
        top = jnp.concatenate([jnp.concatenate([rows[g][t] for t in tiles], axis=1) for g in range(8)], axis=0)
        spans = []
        for half in range(first // 128, 2):
            begin = max(first, 128 * half)
            end = 128 * half + 128
            if begin == first and True:
                spans.append((half, begin, begin + 64))
                begin += 64
            if begin < end:
                spans.append((half, begin, end))
        turned = {half: top[:, 128 * (half - td):128 * (half - td) + 128].T for half in range(first // 128, 2)}
        for half, begin, end in spans:
            use = top if half == td else top[:, 128:]
            delta = jnp.dot(turned[half][begin - 128 * half:end - 128 * half, :], use, precision=HI, preferred_element_type=F32)
            lo = 128 * tiles[0] if half == td else 128 * tiles[1]
            hi = 128 * (tiles[-1] + 1)
            m_ref[begin:end, lo:hi] = m_ref[begin:end, lo:hi] - delta


def chol_fields(gram_ref, low_ref, high_ref, out_ref, upper_ref, m_ref, *, cells):
    row = iota((128, 128), 0)
    col = iota((128, 128), 1)
    eye = jnp.where(row == col, 1.0, 0.0).astype(F32)
    blank = jnp.zeros((128, 128), F32)
    packed = gram_ref[...] * (1.0 / cells)
    folded = packed[0:128]
    mirrored = folded.T
    m_ref[0:128, 0:128] = jnp.where(row >= col, folded, mirrored)
    m_ref[128:256, 0:128] = packed[128:256]
    m_ref[0:128, 128:256] = packed[128:256].T
    m_ref[128:256, 128:256] = jnp.where(row < col, folded, jnp.where(row > col, mirrored, packed[256:257]))
    m_ref[0:128, 256:384] = eye
    m_ref[0:128, 384:512] = blank
    m_ref[128:256, 256:384] = blank
    m_ref[128:256, 384:512] = eye
    eliminate(m_ref)
    upper_ref[0:128, 0:128] = jnp.where(row <= col, m_ref[0:128, 0:128], 0.0)
    upper_ref[0:128, 128:256] = m_ref[0:128, 128:256]
    upper_ref[128:256, 0:128] = blank
    upper_ref[128:256, 128:256] = jnp.where(row <= col, m_ref[128:256, 128:256], 0.0)
    first = jnp.where(row >= col, m_ref[0:128, 256:384], 0.0)
    second = jnp.concatenate([m_ref[128:256, 256:384], jnp.where(row >= col, m_ref[128:256, 384:512], 0.0)], axis=1)
    inverse = jnp.concatenate([jnp.concatenate([first, blank], axis=1), second], axis=0)
    for half, ref in enumerate((low_ref, high_ref)):
        for c in range(0, 6, 2):
            both = jnp.concatenate([ref[c], ref[c + 1]], axis=1)
            y = jnp.dot(inverse, both, precision=HI, preferred_element_type=F32)
            for k in range(2):
                r, f = divmod(c + k, 3)
                out_ref[pl.ds(4 * f + 2 * half + r, 256, stride=12), :] = y[:, 128 * k:128 * k + 128]


def on_chip(*shapes):
    return tuple(pltpu.VMEM(s, F32) for s in shapes)


def kernel(body, out_shape, *args, scratch=(), flags=None):
    args = [pltpu.with_memory_space_constraint(a, pltpu.VMEM) for a in args]
    specs = [pl.BlockSpec(memory_space=pltpu.VMEM)] * len(args)
    if flags is not None:
        args = [flags] + args
        specs = [pl.BlockSpec(memory_space=pltpu.SMEM)] + specs
    out_specs = tuple(pl.BlockSpec(memory_space=pltpu.VMEM) for _ in out_shape)
    return pl.pallas_call(
        body, out_shape=out_shape, in_specs=specs, out_specs=out_specs,
        scratch_shapes=[pltpu.VMEM(s, F32) for s in scratch],
        compiler_params=pltpu.CompilerParams(vmem_limit_bytes=16 * 2**20),
    )(*args)


def per_device(tangent, base_state):
    n_lat = lax.axis_size("lat")
    n_lon = lax.axis_size("lon")
    x = tangent.reshape(3072, 128)
    base = base_state.reshape(16, 128)
    low, high, pack = pl.pallas_call(
        split_rows, out_shape=on_chip((1544, 128), (1544, 128), (264, 128)),
        in_specs=[pl.BlockSpec(memory_space=pl.ANY)] * 2,
        out_specs=(pl.BlockSpec(memory_space=pltpu.VMEM),) * 3,
        scratch_shapes=[pltpu.VMEM((3072, 128), F32), pltpu.VMEM((16, 128), F32), pltpu.SemaphoreType.DMA((5,))],
        compiler_params=pltpu.CompilerParams(vmem_limit_bytes=16 * 2**20),
    )(*[pltpu.with_memory_space_constraint(a, pltpu.HBM) for a in (x, base)])
    east_ring = [(i, (i + 1) % n_lon) for i in range(n_lon)]
    west_ring = [(j, i) for i, j in east_ring]
    north_line = [(i, i + 1) for i in range(n_lat - 1)]
    south_line = [(j, i) for i, j in north_line]
    south = lax.ppermute(high, "lat", north_line)
    west = lax.ppermute(pack, "lon", east_ring)
    east = lax.ppermute(pack, "lon", west_ring)
    north = lax.ppermute(low, "lat", south_line)
    corner_up, corner_down = kernel(corners_out, on_chip((8, 256), (8, 256)), west, east)
    south_corner = lax.ppermute(corner_up, "lat", north_line)
    north_corner = lax.ppermute(corner_down, "lat", south_line)
    part_low, part_high = kernel(
        own_part, on_chip((6, 256, 128), (6, 256, 128)), base, low, high, pack, west, east, scratch=[(20, 8, 128), (12, 256, 128), (3, 256, 128)]
    )
    index = lax.axis_index("lat")
    inside = jnp.stack([index > 0, index < n_lat - 1]).astype(jnp.int32)
    scratch = [(16, 8, 128), (256, 128)]
    s_low, gram = kernel(
        south_side, on_chip((6, 256, 128), (256, 256)),
        base, low, south, pack, west, east, south_corner, part_low, scratch=scratch, flags=inside,
    )
    s_high, gram = kernel(
        north_side, on_chip((6, 256, 128), (272, 128)),
        base, high, north, pack, west, east, north_corner, part_high, gram, scratch=scratch, flags=inside,
    )
    gram = lax.all_to_all(gram.reshape(n_lon, 1, -1), "lon", 0, 0, tiled=True)
    (gram,) = kernel(sum_copies, on_chip((n_lat,) + gram.shape[1:]), gram)
    gram = lax.all_to_all(gram, "lat", 0, 0, tiled=True)
    (gram,) = kernel(sum_copies, on_chip((n_lon,) + gram.shape[1:]), gram)
    gram = lax.all_to_all(gram, "lon", 0, 0, tiled=True)
    cells = 4 * 128 * n_lat * n_lon
    fields, upper = kernel(
        lambda *refs: chol_fields(*refs, cells=cells),
        tuple(jax.ShapeDtypeStruct(s, F32) for s in ((3072, 128), (256, 256))),
        gram.reshape(272, 128), s_low, s_high, scratch=[(256, 512)],
    )
    return (fields.reshape(tangent.shape), upper)


def solution(mesh):
    in_specs = (P(None, None, "lat", "lon"), P(None, "lat", "lon"))
    out_specs = (P(None, None, "lat", "lon"), P())
    return jax.shard_map(
        per_device, mesh=mesh, in_specs=in_specs, out_specs=out_specs, check_vma=False
    )
```

profile of v0, /device:TPU:1, one launch (start us, length us, event | category | flops | bytes accessed | tf_op | source)
XLA Modules:
  0.0 101.6 jit_solution(4122863844716739131)
XLA Ops:
  0.6 0.0 copy-start
  0.6 2.7 %shard_map.41 = (f32[1544,128]{1,0:T(8,128)S(1)}, f32[1544,128]{1,0:T(8,128)S(1)}, f32[264,128]{1,0:T(8,128)S(1)}) custom-call(f32[3072,128]{1,0:T(8,128)} %bitcast.13, f32[16,128]{1,0:T(8,128)} %bitcast.9), custom_call_target="tpu_custom_call" | custom-call | tf_op jit(solution)/shard_map/pallas_call | solution.py:413
  3.4 5.7 %collective-permute-start.4 = (f32[1544,128]{1,0:T(8,128)S(1)}, f32[1544,128]{1,0:T(8,128)}, u32[]{:S(2)}, u32[]{:S(2)}) collective-permute-start(f32[1544,128]{1,0:T(8,128)S(1)} %get-tuple-element.15.high_ref.half_ref), channel_id=1, source_target_pairs={{0,16},{16,32},{32,48},{48,64},{64,80},{80,96},{96,112},{112,128},... | collective-permute-start | bytes 2371592 | tf_op jit(solution)/shard_map/ppermute | solution.py:424
  9.1 1.3 %collective-permute-start = (f32[1544,128]{1,0:T(8,128)S(1)}, f32[1544,128]{1,0:T(8,128)S(1)}, u32[]{:S(2)}, u32[]{:S(2)}) collective-permute-start(f32[1544,128]{1,0:T(8,128)S(1)} %get-tuple-element.16.low_ref.half_ref), channel_id=1, source_target_pairs={{16,0},{32,16},{48,32},{64,48},{80,64},{96,80},{112,96},{128,112},... | collective-permute-start | bytes 2371592 | tf_op jit(solution)/shard_map/ppermute | solution.py:427
  10.4 2.1 %collective-permute-start.1 = (f32[264,128]{1,0:T(8,128)S(1)}, f32[264,128]{1,0:T(8,128)S(1)}, u32[]{:S(2)}, u32[]{:S(2)}) collective-permute-start(f32[264,128]{1,0:T(8,128)S(1)} %get-tuple-element.17.pack_ref), channel_id=1, source_target_pairs={{0,1},{1,2},{2,3},{3,4},{4,5},{5,6},{6,7},{7,8},{8,9},{9,10},{10,1... | collective-permute-start | bytes 405512 | tf_op jit(solution)/shard_map/ppermute | solution.py:425
  12.5 1.2 %collective-permute-start.2 = (f32[264,128]{1,0:T(8,128)S(1)}, f32[264,128]{1,0:T(8,128)S(1)}, u32[]{:S(2)}, u32[]{:S(2)}) collective-permute-start(f32[264,128]{1,0:T(8,128)S(1)} %get-tuple-element.17.pack_ref), channel_id=1, source_target_pairs={{1,0},{2,1},{3,2},{4,3},{5,4},{6,5},{7,6},{8,7},{9,8},{10,9},{11,1... | collective-permute-start | bytes 405512 | tf_op jit(solution)/shard_map/ppermute | solution.py:426
  13.7 0.8 collective-permute-done.1.west_ref
  14.5 2.4 %collective-permute-done.2.east_ref = f32[264,128]{1,0:T(8,128)S(1)} collective-permute-done((f32[264,128]{1,0:T(8,128)S(1)}, f32[264,128]{1,0:T(8,128)S(1)}, u32[]{:S(2)}, u32[]{:S(2)}) %collective-permute-start.2) | collective-permute-done | bytes 135200 | tf_op jit(solution)/shard_map/ppermute | solution.py:426
  17.0 0.3 shard_map.42
  17.3 4.7 %collective-permute-start.5 = (f32[8,256]{1,0:T(8,128)S(1)}, f32[8,256]{1,0:T(8,128)S(1)}, u32[]{:S(2)}, u32[]{:S(2)}) collective-permute-start(f32[8,256]{1,0:T(8,128)S(1)} %get-tuple-element.20), channel_id=1, source_target_pairs={{0,16},{16,32},{32,48},{48,64},{64,80},{80,96},{96,112},{112,128},... | collective-permute-start | bytes 24584 | tf_op jit(solution)/shard_map/ppermute | solution.py:429
  21.9 1.3 %collective-permute-start.3 = (f32[8,256]{1,0:T(8,128)S(1)}, f32[8,256]{1,0:T(8,128)S(1)}, u32[]{:S(2)}, u32[]{:S(2)}) collective-permute-start(f32[8,256]{1,0:T(8,128)S(1)} %get-tuple-element.18), channel_id=1, source_target_pairs={{16,0},{32,16},{48,32},{64,48},{80,64},{96,80},{112,96},{128,112},... | collective-permute-start | bytes 24584 | tf_op jit(solution)/shard_map/ppermute | solution.py:430
  23.2 0.1 add_convert_fusion.inside_ref
  23.3 0.0 copy-done
  23.3 5.4 %shard_map.43 = (f32[6,256,128]{2,1,0:T(8,128)S(1)}, f32[6,256,128]{2,1,0:T(8,128)S(1)}) custom-call(f32[16,128]{1,0:T(8,128)S(1)} %bitcast.10, f32[1544,128]{1,0:T(8,128)S(1)} %get-tuple-element.16.low_ref.half_ref, f32[1544,128]{1,0:T(8,128)S(1)} %get-tuple-element.15.high_ref.half_ref, f32[264,128]{1,0:T(8,128)S(1)} %get-tuple-element.17.pack_ref, ...), custom_call_target="tpu_custom_call" | custom-call | tf_op jit(solution)/shard_map/pallas_call | solution.py:401
  28.7 0.0 collective-permute-done.5.corner_ref
  28.7 0.0 collective-permute-done.4.halo_ref
  28.7 4.6 %shard_map.44 = (f32[6,256,128]{2,1,0:T(8,128)S(1)}, f32[256,256]{1,0:T(8,128)S(1)}) custom-call(s32[2]{0:T(128)S(1)} %add_convert_fusion.inside_ref, f32[16,128]{1,0:T(8,128)S(1)} %bitcast.11, f32[1544,128]{1,0:T(8,128)S(1)} %get-tuple-element.16.low_ref.half_ref, f32[1544,128]{1,0:T(8,128)} %collective-permute-done.4.halo_ref, ...), custom_call_target="tpu_custom_call" | custom-call | tf_op jit(solution)/shard_map/pallas_call | solution.py:401
  33.4 0.0 collective-permute-done.3.corner_ref
  33.4 0.0 collective-permute-done.halo_ref
  33.4 2.7 %shard_map.45 = (f32[6,256,128]{2,1,0:T(8,128)S(1)}, f32[272,128]{1,0:T(8,128)S(1)}) custom-call(s32[2]{0:T(128)S(1)} %add_convert_fusion.inside_ref, f32[16,128]{1,0:T(8,128)S(1)} %bitcast.12, f32[1544,128]{1,0:T(8,128)S(1)} %get-tuple-element.15.high_ref.half_ref, f32[1544,128]{1,0:T(8,128)S(1)} %collective-permute-done.halo_ref, ...), custom_call_target="tpu_custom_call" | custom-call | tf_op jit(solution)/shard_map/pallas_call | solution.py:401
  36.1 15.9 %all_to_all.15.in_ref = f32[16,1,2176]{2,1,0:T(1,128)S(1)} all-to-all(f32[16,1,2176]{2,1,0:T(1,128)S(1)} %bitcast.8), channel_id=1, replica_groups=mesh['lat'=32,'lon'=16] {'lon'}, dimensions={0} | all-to-all | bytes 278528 | tf_op jit(solution)/shard_map/all_to_all | solution.py:445
  52.0 25.2 %all_to_all.16.in_ref = f32[32,1,2176]{2,1,0:T(1,128)S(1)} all-to-all(f32[32,1,2176]{2,1,0:T(1,128)S(1)} %shard_map.46), channel_id=1, replica_groups=mesh['lat'=32,'lon'=16] {'lat'}, dimensions={0} | all-to-all | bytes 557056 | tf_op jit(solution)/shard_map/all_to_all | solution.py:447
  77.2 14.4 %all_to_all.17 = f32[16,1,2176]{2,1,0:T(1,128)S(1)} all-to-all(f32[16,1,2176]{2,1,0:T(1,128)S(1)} %shard_map.47), channel_id=1, replica_groups=mesh['lat'=32,'lon'=16] {'lon'}, dimensions={0} | all-to-all | bytes 278528 | tf_op jit(solution)/shard_map/all_to_all | solution.py:449
  91.7 9.9 %shard_map.48 = (f32[3072,128]{1,0:T(8,128)}, f32[256,256]{1,0:T(8,128)}) custom-call(f32[272,128]{1,0:T(8,128)S(1)} %bitcast.7, f32[6,256,128]{2,1,0:T(8,128)S(1)} %get-tuple-element.24.refs_1_, f32[6,256,128]{2,1,0:T(8,128)S(1)} %get-tuple-element.25.refs_2_), custom_call_target="tpu_custom_call" | custom-call | tf_op jit(solution)/shard_map/pallas_call | solution.py:401
  (2 shorter events, 0.1 us)
Async XLA Ops:
  0.6 22.7 %copy-start = (f32[4,4,128]{2,1,0:T(4,128)S(1)}, f32[4,4,128]{2,1,0:T(4,128)}, u32[]{:S(2)}) copy-start(f32[4,4,128]{2,1,0:T(4,128)} %param.3) | copy-start | bytes 24580
  3.4 25.4 %collective-permute-start.4 = (f32[1544,128]{1,0:T(8,128)S(1)}, f32[1544,128]{1,0:T(8,128)}, u32[]{:S(2)}, u32[]{:S(2)}) collective-permute-start(f32[1544,128]{1,0:T(8,128)S(1)} %get-tuple-element.15.high_ref.half_ref), channel_id=1, source_target_pairs={{0,16},{16,32},{32,48},{48,64},{64,80},{80,96},{96,112},{112,128},... | collective-permute-start | bytes 2371592 | tf_op jit(solution)/shard_map/ppermute | solution.py:424
  9.1 24.3 %collective-permute-start = (f32[1544,128]{1,0:T(8,128)S(1)}, f32[1544,128]{1,0:T(8,128)S(1)}, u32[]{:S(2)}, u32[]{:S(2)}) collective-permute-start(f32[1544,128]{1,0:T(8,128)S(1)} %get-tuple-element.16.low_ref.half_ref), channel_id=1, source_target_pairs={{16,0},{32,16},{48,32},{64,48},{80,64},{96,80},{112,96},{128,112},... | collective-permute-start | bytes 2371592 | tf_op jit(solution)/shard_map/ppermute | solution.py:427
  10.4 4.2 %collective-permute-start.1 = (f32[264,128]{1,0:T(8,128)S(1)}, f32[264,128]{1,0:T(8,128)S(1)}, u32[]{:S(2)}, u32[]{:S(2)}) collective-permute-start(f32[264,128]{1,0:T(8,128)S(1)} %get-tuple-element.17.pack_ref), channel_id=1, source_target_pairs={{0,1},{1,2},{2,3},{3,4},{4,5},{5,6},{6,7},{7,8},{8,9},{9,10},{10,1... | collective-permute-start | bytes 405512 | tf_op jit(solution)/shard_map/ppermute | solution.py:425
  12.5 4.4 %collective-permute-start.2 = (f32[264,128]{1,0:T(8,128)S(1)}, f32[264,128]{1,0:T(8,128)S(1)}, u32[]{:S(2)}, u32[]{:S(2)}) collective-permute-start(f32[264,128]{1,0:T(8,128)S(1)} %get-tuple-element.17.pack_ref), channel_id=1, source_target_pairs={{1,0},{2,1},{3,2},{4,3},{5,4},{6,5},{7,6},{8,7},{9,8},{10,9},{11,1... | collective-permute-start | bytes 405512 | tf_op jit(solution)/shard_map/ppermute | solution.py:426
  17.3 11.5 %collective-permute-start.5 = (f32[8,256]{1,0:T(8,128)S(1)}, f32[8,256]{1,0:T(8,128)S(1)}, u32[]{:S(2)}, u32[]{:S(2)}) collective-permute-start(f32[8,256]{1,0:T(8,128)S(1)} %get-tuple-element.20), channel_id=1, source_target_pairs={{0,16},{16,32},{32,48},{48,64},{64,80},{80,96},{96,112},{112,128},... | collective-permute-start | bytes 24584 | tf_op jit(solution)/shard_map/ppermute | solution.py:429
  21.9 11.4 %collective-permute-start.3 = (f32[8,256]{1,0:T(8,128)S(1)}, f32[8,256]{1,0:T(8,128)S(1)}, u32[]{:S(2)}, u32[]{:S(2)}) collective-permute-start(f32[8,256]{1,0:T(8,128)S(1)} %get-tuple-element.18), channel_id=1, source_target_pairs={{16,0},{32,16},{48,32},{64,48},{80,64},{96,80},{112,96},{128,112},... | collective-permute-start | bytes 24584 | tf_op jit(solution)/shard_map/ppermute | solution.py:430
where the time goes:
time: 102 us
  blocking collectives  55.5 us (54%)
  Pallas kernels  25.7 us (25%)
  starting transfers between devices  16.3 us (16%)
  waiting for transfers between devices  3.24 us (3%)
    all_to_all x1, blocking collectives, per_device(): gram = lax.all_to_all(gram, 'lat', 0, 0, tiled=True)  25.2 us
    pallas_call x7, Pallas kernels, kernel(): pl.pallas_call(body, out_shape=out_shape, in_specs=specs, out_specs=out_s...  23 us
    all_to_all x1, blocking collectives, per_device(): gram = lax.all_to_all(gram.reshape(n_lon, 1, -1), 'lon', 0, 0, tiled=True)  15.9 us
    all_to_all x1, blocking collectives, per_device(): gram = lax.all_to_all(gram, 'lon', 0, 0, tiled=True)  14.4 us
    ppermute x1, starting transfers between devices, per_device(): south = lax.ppermute(high, 'lat', north_line)  5.71 us
    ppermute x1, starting transfers between devices, per_device(): south_corner = lax.ppermute(corner_up, 'lat', north_line)  4.69 us
    pallas_call x1, Pallas kernels, per_device(): pl.pallas_call(split_rows, out_shape=on_chip((1544, 128), (1544, 128), (2...  2.73 us
    ppermute x1, waiting for transfers between devices, per_device(): east = lax.ppermute(pack, 'lon', west_ring)  2.41 us
  transfers between devices with their start and end apart: 6, of which 2 were waited for; matrix products, arithmetic and copies ran while one was open for 0% of the time, Pallas kernels for 10%

commit v1 on v0

--- a/solution.py
+++ b/solution.py
@@ -354,7 +354,7 @@
             m_ref[begin:end, lo:hi] = m_ref[begin:end, lo:hi] - delta
 
 
-def chol_fields(gram_ref, low_ref, high_ref, out_ref, upper_ref, m_ref, *, cells):
+def chol_fields(gram_ref, low_ref, high_ref, out_hbm, upper_ref, m_ref, out_ref, sems, *, cells):
     row = iota((128, 128), 0)
     col = iota((128, 128), 1)
     eye = jnp.where(row == col, 1.0, 0.0).astype(F32)
@@ -371,20 +371,27 @@
     m_ref[128:256, 256:384] = blank
     m_ref[128:256, 384:512] = eye
     eliminate(m_ref)
+    first = jnp.where(row >= col, m_ref[0:128, 256:384], 0.0)
+    second = jnp.concatenate([m_ref[128:256, 256:384], jnp.where(row >= col, m_ref[128:256, 384:512], 0.0)], axis=1)
+    copies = []
+    for k, inverse in enumerate((first, second)):
+        for half, ref in enumerate((low_ref, high_ref)):
+            for c in range(0, 6, 2):
+                both = jnp.concatenate([ref[c, 0:128 * k + 128, :], ref[c + 1, 0:128 * k + 128, :]], axis=1)
+                y = jnp.dot(inverse, both, precision=HI, preferred_element_type=F32)
+                for j in range(2):
+                    r, f = divmod(c + j, 3)
+                    place = pl.ds(1536 * k + 4 * f + 2 * half + r, 128, stride=12)
+                    out_ref[place, :] = y[:, 128 * j:128 * j + 128]
+        place = pl.ds(1536 * k, 1536)
+        copies.append(pltpu.make_async_copy(out_ref.at[place], out_hbm.at[place], sems.at[k]))
+        copies[k].start()
     upper_ref[0:128, 0:128] = jnp.where(row <= col, m_ref[0:128, 0:128], 0.0)
     upper_ref[0:128, 128:256] = m_ref[0:128, 128:256]
     upper_ref[128:256, 0:128] = blank
     upper_ref[128:256, 128:256] = jnp.where(row <= col, m_ref[128:256, 128:256], 0.0)
-    first = jnp.where(row >= col, m_ref[0:128, 256:384], 0.0)
-    second = jnp.concatenate([m_ref[128:256, 256:384], jnp.where(row >= col, m_ref[128:256, 384:512], 0.0)], axis=1)
-    inverse = jnp.concatenate([jnp.concatenate([first, blank], axis=1), second], axis=0)
-    for half, ref in enumerate((low_ref, high_ref)):
-        for c in range(0, 6, 2):
-            both = jnp.concatenate([ref[c], ref[c + 1]], axis=1)
-            y = jnp.dot(inverse, both, precision=HI, preferred_element_type=F32)
-            for k in range(2):
-                r, f = divmod(c + k, 3)
-                out_ref[pl.ds(4 * f + 2 * half + r, 256, stride=12), :] = y[:, 128 * k:128 * k + 128]
+    for copy in copies:
+        copy.wait()
 
 
 def on_chip(*shapes):
@@ -448,11 +455,15 @@
     (gram,) = kernel(sum_copies, on_chip((n_lon,) + gram.shape[1:]), gram)
     gram = lax.all_to_all(gram, "lon", 0, 0, tiled=True)
     cells = 4 * 128 * n_lat * n_lon
-    fields, upper = kernel(
+    args = [pltpu.with_memory_space_constraint(a, pltpu.VMEM) for a in (gram.reshape(272, 128), s_low, s_high)]
+    vmem = pl.BlockSpec(memory_space=pltpu.VMEM)
+    fields, upper = pl.pallas_call(
         lambda *refs: chol_fields(*refs, cells=cells),
-        tuple(jax.ShapeDtypeStruct(s, F32) for s in ((3072, 128), (256, 256))),
-        gram.reshape(272, 128), s_low, s_high, scratch=[(256, 512)],
-    )
+        out_shape=tuple(jax.ShapeDtypeStruct(s, F32) for s in ((3072, 128), (256, 256))),
+        in_specs=[vmem] * 3, out_specs=(pl.BlockSpec(memory_space=pl.ANY), vmem),
+        scratch_shapes=[pltpu.VMEM((256, 512), F32), pltpu.VMEM((3072, 128), F32), pltpu.SemaphoreType.DMA((2,))],
+        compiler_params=pltpu.CompilerParams(vmem_limit_bytes=16 * 2**20),
+    )(*args)
     return (fields.reshape(tangent.shape), upper)
 
 

time: 102 us -> 102 us (level)
    pallas_call x0 -> x1, Pallas kernels: none -> 9.95 us  [per_device(): pl.pallas_call(lambda *refs: chol_fields(*refs, cells=cells), out_shape=t...]
    pallas_call x7 -> x6, Pallas kernels: 23 us -> 13.1 us  [kernel(): pl.pallas_call(body, out_shape=out_shape, in_specs=specs, out_specs=out_s...]
where the time goes in v1:
time: 102 us
  blocking collectives  55.5 us (54%)
  Pallas kernels  25.7 us (25%)
  starting transfers between devices  16.3 us (16%)
  waiting for transfers between devices  3.24 us (3%)
    all_to_all x1, blocking collectives, per_device(): gram = lax.all_to_all(gram, 'lat', 0, 0, tiled=True)  25.2 us
    all_to_all x1, blocking collectives, per_device(): gram = lax.all_to_all(gram.reshape(n_lon, 1, -1), 'lon', 0, 0, tiled=True)  15.9 us
    all_to_all x1, blocking collectives, per_device(): gram = lax.all_to_all(gram, 'lon', 0, 0, tiled=True)  14.4 us
    pallas_call x6, Pallas kernels, kernel(): pl.pallas_call(body, out_shape=out_shape, in_specs=specs, out_specs=out_s...  13.1 us
    pallas_call x1, Pallas kernels, per_device(): pl.pallas_call(lambda *refs: chol_fields(*refs, cells=cells), out_shape=t...  9.95 us
    ppermute x1, starting transfers between devices, per_device(): south = lax.ppermute(high, 'lat', north_line)  5.71 us
    ppermute x1, starting transfers between devices, per_device(): south_corner = lax.ppermute(corner_up, 'lat', north_line)  4.69 us
    pallas_call x1, Pallas kernels, per_device(): pl.pallas_call(split_rows, out_shape=on_chip((1544, 128), (1544, 128), (2...  2.73 us
  transfers between devices with their start and end apart: 6, of which 2 were waited for; matrix products, arithmetic and copies ran while one was open for 0% of the time, Pallas kernels for 10%

profile of v1, /device:TPU:1, one launch (start us, length us, event | category | flops | bytes accessed | tf_op | source)
XLA Modules:
  0.0 101.8 jit_solution(4133435300216770896)
XLA Ops:
  0.6 0.0 copy-start
  0.6 2.7 %shard_map.41 = (f32[1544,128]{1,0:T(8,128)S(1)}, f32[1544,128]{1,0:T(8,128)S(1)}, f32[264,128]{1,0:T(8,128)S(1)}) custom-call(f32[3072,128]{1,0:T(8,128)} %bitcast.13, f32[16,128]{1,0:T(8,128)} %bitcast.9), custom_call_target="tpu_custom_call" | custom-call | tf_op jit(solution)/shard_map/pallas_call | solution.py:420
  3.4 5.7 %collective-permute-start.4 = (f32[1544,128]{1,0:T(8,128)S(1)}, f32[1544,128]{1,0:T(8,128)}, u32[]{:S(2)}, u32[]{:S(2)}) collective-permute-start(f32[1544,128]{1,0:T(8,128)S(1)} %get-tuple-element.15.high_ref.half_ref), channel_id=1, source_target_pairs={{0,16},{16,32},{32,48},{48,64},{64,80},{80,96},{96,112},{112,128},... | collective-permute-start | bytes 2371592 | tf_op jit(solution)/shard_map/ppermute | solution.py:431
  9.1 1.3 %collective-permute-start = (f32[1544,128]{1,0:T(8,128)S(1)}, f32[1544,128]{1,0:T(8,128)S(1)}, u32[]{:S(2)}, u32[]{:S(2)}) collective-permute-start(f32[1544,128]{1,0:T(8,128)S(1)} %get-tuple-element.16.low_ref.half_ref), channel_id=1, source_target_pairs={{16,0},{32,16},{48,32},{64,48},{80,64},{96,80},{112,96},{128,112},... | collective-permute-start | bytes 2371592 | tf_op jit(solution)/shard_map/ppermute | solution.py:434
  10.4 2.1 %collective-permute-start.1 = (f32[264,128]{1,0:T(8,128)S(1)}, f32[264,128]{1,0:T(8,128)S(1)}, u32[]{:S(2)}, u32[]{:S(2)}) collective-permute-start(f32[264,128]{1,0:T(8,128)S(1)} %get-tuple-element.17.pack_ref), channel_id=1, source_target_pairs={{0,1},{1,2},{2,3},{3,4},{4,5},{5,6},{6,7},{7,8},{8,9},{9,10},{10,1... | collective-permute-start | bytes 405512 | tf_op jit(solution)/shard_map/ppermute | solution.py:432
  12.5 1.2 %collective-permute-start.2 = (f32[264,128]{1,0:T(8,128)S(1)}, f32[264,128]{1,0:T(8,128)S(1)}, u32[]{:S(2)}, u32[]{:S(2)}) collective-permute-start(f32[264,128]{1,0:T(8,128)S(1)} %get-tuple-element.17.pack_ref), channel_id=1, source_target_pairs={{1,0},{2,1},{3,2},{4,3},{5,4},{6,5},{7,6},{8,7},{9,8},{10,9},{11,1... | collective-permute-start | bytes 405512 | tf_op jit(solution)/shard_map/ppermute | solution.py:433
  13.7 0.8 collective-permute-done.1.west_ref
  14.5 2.4 %collective-permute-done.2.east_ref = f32[264,128]{1,0:T(8,128)S(1)} collective-permute-done((f32[264,128]{1,0:T(8,128)S(1)}, f32[264,128]{1,0:T(8,128)S(1)}, u32[]{:S(2)}, u32[]{:S(2)}) %collective-permute-start.2) | collective-permute-done | bytes 135200 | tf_op jit(solution)/shard_map/ppermute | solution.py:433
  17.0 0.3 shard_map.42
  17.3 4.7 %collective-permute-start.5 = (f32[8,256]{1,0:T(8,128)S(1)}, f32[8,256]{1,0:T(8,128)S(1)}, u32[]{:S(2)}, u32[]{:S(2)}) collective-permute-start(f32[8,256]{1,0:T(8,128)S(1)} %get-tuple-element.20), channel_id=1, source_target_pairs={{0,16},{16,32},{32,48},{48,64},{64,80},{80,96},{96,112},{112,128},... | collective-permute-start | bytes 24584 | tf_op jit(solution)/shard_map/ppermute | solution.py:436
  21.9 1.3 %collective-permute-start.3 = (f32[8,256]{1,0:T(8,128)S(1)}, f32[8,256]{1,0:T(8,128)S(1)}, u32[]{:S(2)}, u32[]{:S(2)}) collective-permute-start(f32[8,256]{1,0:T(8,128)S(1)} %get-tuple-element.18), channel_id=1, source_target_pairs={{16,0},{32,16},{48,32},{64,48},{80,64},{96,80},{112,96},{128,112},... | collective-permute-start | bytes 24584 | tf_op jit(solution)/shard_map/ppermute | solution.py:437
  23.2 0.1 add_convert_fusion.inside_ref
  23.3 0.0 copy-done
  23.3 5.4 %shard_map.43 = (f32[6,256,128]{2,1,0:T(8,128)S(1)}, f32[6,256,128]{2,1,0:T(8,128)S(1)}) custom-call(f32[16,128]{1,0:T(8,128)S(1)} %bitcast.10, f32[1544,128]{1,0:T(8,128)S(1)} %get-tuple-element.16.low_ref.half_ref, f32[1544,128]{1,0:T(8,128)S(1)} %get-tuple-element.15.high_ref.half_ref, f32[264,128]{1,0:T(8,128)S(1)} %get-tuple-element.17.pack_ref, ...), custom_call_target="tpu_custom_call" | custom-call | tf_op jit(solution)/shard_map/pallas_call | solution.py:408
  28.7 0.0 collective-permute-done.5.corner_ref
  28.7 0.0 collective-permute-done.4.halo_ref
  28.7 4.6 %shard_map.44 = (f32[6,256,128]{2,1,0:T(8,128)S(1)}, f32[256,256]{1,0:T(8,128)S(1)}) custom-call(s32[2]{0:T(128)S(1)} %add_convert_fusion.inside_ref, f32[16,128]{1,0:T(8,128)S(1)} %bitcast.11, f32[1544,128]{1,0:T(8,128)S(1)} %get-tuple-element.16.low_ref.half_ref, f32[1544,128]{1,0:T(8,128)} %collective-permute-done.4.halo_ref, ...), custom_call_target="tpu_custom_call" | custom-call | tf_op jit(solution)/shard_map/pallas_call | solution.py:408
  33.4 0.0 collective-permute-done.3.corner_ref
  33.4 0.0 collective-permute-done.halo_ref
  33.4 2.7 %shard_map.45 = (f32[6,256,128]{2,1,0:T(8,128)S(1)}, f32[272,128]{1,0:T(8,128)S(1)}) custom-call(s32[2]{0:T(128)S(1)} %add_convert_fusion.inside_ref, f32[16,128]{1,0:T(8,128)S(1)} %bitcast.12, f32[1544,128]{1,0:T(8,128)S(1)} %get-tuple-element.15.high_ref.half_ref, f32[1544,128]{1,0:T(8,128)S(1)} %collective-permute-done.halo_ref, ...), custom_call_target="tpu_custom_call" | custom-call | tf_op jit(solution)/shard_map/pallas_call | solution.py:408
  36.1 15.9 %all_to_all.15.in_ref = f32[16,1,2176]{2,1,0:T(1,128)S(1)} all-to-all(f32[16,1,2176]{2,1,0:T(1,128)S(1)} %bitcast.8), channel_id=1, replica_groups=mesh['lat'=32,'lon'=16] {'lon'}, dimensions={0} | all-to-all | bytes 278528 | tf_op jit(solution)/shard_map/all_to_all | solution.py:452
  52.0 25.2 %all_to_all.16.in_ref = f32[32,1,2176]{2,1,0:T(1,128)S(1)} all-to-all(f32[32,1,2176]{2,1,0:T(1,128)S(1)} %shard_map.46), channel_id=1, replica_groups=mesh['lat'=32,'lon'=16] {'lat'}, dimensions={0} | all-to-all | bytes 557056 | tf_op jit(solution)/shard_map/all_to_all | solution.py:454
  77.2 14.4 %all_to_all.17 = f32[16,1,2176]{2,1,0:T(1,128)S(1)} all-to-all(f32[16,1,2176]{2,1,0:T(1,128)S(1)} %shard_map.47), channel_id=1, replica_groups=mesh['lat'=32,'lon'=16] {'lon'}, dimensions={0} | all-to-all | bytes 278528 | tf_op jit(solution)/shard_map/all_to_all | solution.py:456
  91.7 10.0 %shard_map.48 = (f32[3072,128]{1,0:T(8,128)}, f32[256,256]{1,0:T(8,128)}) custom-call(f32[272,128]{1,0:T(8,128)S(1)} %bitcast.7, f32[6,256,128]{2,1,0:T(8,128)S(1)} %get-tuple-element.24.refs_1_, f32[6,256,128]{2,1,0:T(8,128)S(1)} %get-tuple-element.25.refs_2_), custom_call_target="tpu_custom_call" | custom-call | tf_op jit(solution)/shard_map/pallas_call | solution.py:460
  (2 shorter events, 0.1 us)
Async XLA Ops:
  0.6 22.7 %copy-start = (f32[4,4,128]{2,1,0:T(4,128)S(1)}, f32[4,4,128]{2,1,0:T(4,128)}, u32[]{:S(2)}) copy-start(f32[4,4,128]{2,1,0:T(4,128)} %param.3) | copy-start | bytes 24580
  3.4 25.4 %collective-permute-start.4 = (f32[1544,128]{1,0:T(8,128)S(1)}, f32[1544,128]{1,0:T(8,128)}, u32[]{:S(2)}, u32[]{:S(2)}) collective-permute-start(f32[1544,128]{1,0:T(8,128)S(1)} %get-tuple-element.15.high_ref.half_ref), channel_id=1, source_target_pairs={{0,16},{16,32},{32,48},{48,64},{64,80},{80,96},{96,112},{112,128},... | collective-permute-start | bytes 2371592 | tf_op jit(solution)/shard_map/ppermute | solution.py:431
  9.1 24.3 %collective-permute-start = (f32[1544,128]{1,0:T(8,128)S(1)}, f32[1544,128]{1,0:T(8,128)S(1)}, u32[]{:S(2)}, u32[]{:S(2)}) collective-permute-start(f32[1544,128]{1,0:T(8,128)S(1)} %get-tuple-element.16.low_ref.half_ref), channel_id=1, source_target_pairs={{16,0},{32,16},{48,32},{64,48},{80,64},{96,80},{112,96},{128,112},... | collective-permute-start | bytes 2371592 | tf_op jit(solution)/shard_map/ppermute | solution.py:434
  10.4 4.2 %collective-permute-start.1 = (f32[264,128]{1,0:T(8,128)S(1)}, f32[264,128]{1,0:T(8,128)S(1)}, u32[]{:S(2)}, u32[]{:S(2)}) collective-permute-start(f32[264,128]{1,0:T(8,128)S(1)} %get-tuple-element.17.pack_ref), channel_id=1, source_target_pairs={{0,1},{1,2},{2,3},{3,4},{4,5},{5,6},{6,7},{7,8},{8,9},{9,10},{10,1... | collective-permute-start | bytes 405512 | tf_op jit(solution)/shard_map/ppermute | solution.py:432
  12.5 4.4 %collective-permute-start.2 = (f32[264,128]{1,0:T(8,128)S(1)}, f32[264,128]{1,0:T(8,128)S(1)}, u32[]{:S(2)}, u32[]{:S(2)}) collective-permute-start(f32[264,128]{1,0:T(8,128)S(1)} %get-tuple-element.17.pack_ref), channel_id=1, source_target_pairs={{1,0},{2,1},{3,2},{4,3},{5,4},{6,5},{7,6},{8,7},{9,8},{10,9},{11,1... | collective-permute-start | bytes 405512 | tf_op jit(solution)/shard_map/ppermute | solution.py:433
  17.3 11.5 %collective-permute-start.5 = (f32[8,256]{1,0:T(8,128)S(1)}, f32[8,256]{1,0:T(8,128)S(1)}, u32[]{:S(2)}, u32[]{:S(2)}) collective-permute-start(f32[8,256]{1,0:T(8,128)S(1)} %get-tuple-element.20), channel_id=1, source_target_pairs={{0,16},{16,32},{32,48},{48,64},{64,80},{80,96},{96,112},{112,128},... | collective-permute-start | bytes 24584 | tf_op jit(solution)/shard_map/ppermute | solution.py:436
  21.9 11.4 %collective-permute-start.3 = (f32[8,256]{1,0:T(8,128)S(1)}, f32[8,256]{1,0:T(8,128)S(1)}, u32[]{:S(2)}, u32[]{:S(2)}) collective-permute-start(f32[8,256]{1,0:T(8,128)S(1)} %get-tuple-element.18), channel_id=1, source_target_pairs={{16,0},{32,16},{48,32},{64,48},{80,64},{96,80},{112,96},{128,112},... | collective-permute-start | bytes 24584 | tf_op jit(solution)/shard_map/ppermute | solution.py:437
